TPU v7x, 32 devices: a whole 2x2x4 slice. The times are simulated.
32 devices in a mesh: groups: 2 (over y), bins: 4 (over z), fdot: 4 (over x, core).
Axes of the slice: x: 2, y: 2, z: 4, core: 2. Of those that a mesh axis runs over, the one named last changes fastest.
Arguments:
- spectrum: float32 [2, 262144], P(None, ('groups', 'bins')), parts along dimension 1, may hold values from -80 to 80
- bank: bfloat16 [128, 2, 128], replicated, may hold values from -0.5 to 0.5
- fdot_index: int32 [32], P('fdot'), may hold values from 0 to 127
- harm_map: int32 [7, 4, 4], P(None, 'bins'), may hold values from 0 to 28672, as said below
Outputs:
- harmonic_power: float32 [32, 262144], P('fdot', ('groups', 'bins')), parts along dimension 1
There are 2 independent parts, one for each index of `groups`. A program takes and returns all parts, laid end to end along the dimension named above; an argument that names none is the same for every part. Nothing has to cross between parts.
Inputs may be any that keep to these rules, and one draw needn't show every extreme that they name: harm_map[q, d] = (floor(d s / 8), s, (d * 32768 s / 8) mod 32768, p) with s = 4, 2, 6, 1, 3, 5, 7 for q = 0 .. 6 and a rounding phase p in 0 .. 7.
All inputs are finite; a program needn't handle non-finite values.
Results may differ from a plain program's by a relative error of at most 0.0003.
The roundings to bfloat16 on the way count: a program that leaves them out, or rounds other values in their place, can miss the bound.
Values may be sent and summed in bfloat16 or wider, within the bound.
A program may use at most 64 MiB of HBM per device.

v0:
```python
import math

import jax
import jax.numpy as jnp
from jax import lax
from jax.experimental import pallas as pl
from jax.experimental.pallas import tpu as pltpu
from jax.sharding import PartitionSpec as P

LANES = 128
STRIDE_TABLE = (4, 2, 6, 1, 3, 5, 7)


def from_behind(value, axis, steps):
    count = lax.axis_size(axis)
    pairs = [(source, (source + steps) % count) for source in range(count)]
    return lax.ppermute(value, axis, pairs)


def from_partner(value, axis, apart):
    mask = 2**apart
    pairs = [(source, source ^ mask) for source in range(lax.axis_size(axis))]
    return lax.ppermute(value, axis, pairs)


def unpack(packed, mirrored, positions, total_bins):
    real_a, imag_a = (packed[0], packed[1])
    real_b, imag_b = (mirrored[0], mirrored[1])
    even_real = 0.5 * (real_a + real_b)
    even_imag = 0.5 * (imag_a - imag_b)
    odd_real = 0.5 * (imag_a + imag_b)
    odd_imag = 0.5 * (real_b - real_a)
    angle = positions.astype(jnp.float32) * jnp.float32(math.pi / total_bins)
    cosine = jnp.cos(angle)
    sine = jnp.sin(angle)
    out_real = even_real + cosine * odd_real + sine * odd_imag
    out_imag = even_imag + cosine * odd_imag - sine * odd_real
    return (out_real, out_imag)


def search_layout(block_rows):
    spans = [(8, 0, block_rows)]
    row = block_rows
    for stride in STRIDE_TABLE:
        count = stride * block_rows // 8 + 16
        spans.append((stride, row, count))
        row += count
    return spans, -(-row // 256) * 256


def search_kernel(block_rows, templates, harm_ref, index_ref, bank_ref, spec_ref, out_ref,
                  lines_ref, window_ref, weight_ref, plane_ref):
    spans, window_rows = search_layout(block_rows)
    total_rows = spec_ref.shape[1]
    position = lax.axis_index("bins")
    n_bank = bank_ref.shape[0]
    lane_of = lax.broadcasted_iota(jnp.int32, (templates, n_bank), 1)
    onehot = jnp.where(index_ref[...] == lane_of, 1.0, 0.0).astype(jnp.bfloat16)
    taps = jnp.dot(onehot, bank_ref[...], preferred_element_type=jnp.float32).astype(jnp.bfloat16)
    tap = lax.broadcasted_iota(jnp.int32, (LANES, 2 * LANES), 0)
    lane = lax.broadcasted_iota(jnp.int32, (LANES, 2 * LANES), 1)
    turn = jnp.where((tap + lane) % (2 * LANES) == 0, 1.0, 0.0).astype(jnp.bfloat16)
    turned = [
        jnp.dot(taps[:, part * LANES : (part + 1) * LANES], turn, preferred_element_type=jnp.float32)
        for part in range(2)
    ]
    for template in range(templates):
        parts = []
        for part in range(2):
            row = jnp.broadcast_to(turned[part][template : template + 1, :], (2 * LANES, 2 * LANES))
            rolled = pltpu.roll(row, 0, 1, stride=1, stride_axis=0)
            parts.append(rolled[:, :LANES].astype(jnp.bfloat16))
        real, imag = parts
        weight_ref[template, : 2 * LANES, :LANES] = real
        weight_ref[template, : 2 * LANES, LANES:] = imag
        weight_ref[template, 2 * LANES :, :LANES] = -imag
        weight_ref[template, 2 * LANES :, LANES:] = real
    low_half = lax.broadcasted_iota(jnp.int32, (1, LANES), 1) < LANES // 2
    for part in range(2):
        lines_ref[part, :8, :] = jnp.zeros((8, LANES), jnp.float32)
        lines_ref[part, pl.ds(8 + total_rows, 8), :] = jnp.zeros((8, LANES), jnp.float32)

        @pl.loop(0, total_rows // 256)
        def _(step, part=part):
            row = pl.multiple_of(step * 256, 256)
            lines_ref[part, pl.ds(row + 8, 256), :] = spec_ref[part, pl.ds(row, 256), :].astype(
                jnp.float32
            )

    for stride, first, count in spans:
        start = position * (stride * block_rows // 8)
        piece = 16
        for part in range(2):

            @pl.loop(0, count // piece)
            def _(step, part=part, first=first, start=start):
                row = pl.multiple_of(step * piece, piece)
                source = pl.multiple_of(start + row, 8)
                before = pltpu.roll(lines_ref[part, pl.ds(source + 7, piece), :], LANES // 2, 1)
                here = pltpu.roll(lines_ref[part, pl.ds(source + 8, piece), :], LANES // 2, 1)
                after = pltpu.roll(lines_ref[part, pl.ds(source + 9, piece), :], LANES // 2, 1)
                target = pl.ds(pl.multiple_of(first + row, piece), piece)
                window_ref[target, pl.ds(2 * part * LANES, LANES)] = jnp.where(
                    low_half, before, here
                ).astype(jnp.bfloat16)
                window_ref[target, pl.ds((2 * part + 1) * LANES, LANES)] = jnp.where(
                    low_half, here, after
                ).astype(jnp.bfloat16)

    used = spans[-1][1] + spans[-1][2]
    if used < window_rows:
        window_ref[used:, :] = jnp.zeros((window_rows - used, 4 * LANES), jnp.bfloat16)

    @pl.loop(0, window_rows // 256)
    def _(step):
        row = pl.multiple_of(step * 256, 256)
        lhs = window_ref[pl.ds(row, 256), :]
        for template in range(templates):
            amps = jnp.dot(lhs, weight_ref[template], preferred_element_type=jnp.float32)
            real, imag = amps[:, :LANES], amps[:, LANES:]
            plane_ref[pl.ds(row * templates + template, 256, stride=templates), :] = (
                real * real + imag * imag
            )

    column = lax.broadcasted_iota(jnp.int32, (templates, LANES), 1)

    @pl.loop(0, block_rows // 8)
    def _(group):
        sums = []
        for unit in range(8):
            row = pl.multiple_of((group * 8 + unit) * templates, templates)
            sums.append(plane_ref[pl.ds(row, templates), :])
        for number, (stride, first, _) in enumerate(spans[1:]):
            base = (column * stride + harm_ref[number, 3]) // 8

            def source_row(line, first=first, stride=stride):
                row = (first + group * stride + line) * templates
                return plane_ref[pl.ds(pl.multiple_of(row, templates), templates), :]

            for unit in range(8):
                begin = unit * stride * (LANES // 8)
                line, offset = begin // LANES, begin % LANES
                where = base + offset
                wrapped = where & (LANES - 1)
                picked = jnp.take_along_axis(source_row(line), wrapped, axis=1)
                if offset + stride * (LANES // 8) >= LANES:
                    follow = jnp.take_along_axis(source_row(line + 1), wrapped, axis=1)
                    picked = jnp.where(where < LANES, picked, follow)
                sums[unit] = sums[unit] + picked
        for unit in range(8):
            row = pl.multiple_of((group * 8 + unit) * templates, templates)
            out_ref[pl.ds(row, templates), :] = sums[unit] * 0.125


def search(normed_rows, bank, fdot_index, harm_map, block_rows):
    own = fdot_index.shape[0]
    templates = -(-own // 8) * 8
    n_bank = bank.shape[0]
    total_rows = normed_rows.shape[1]
    spans, window_rows = search_layout(block_rows)
    index = jnp.pad(fdot_index, (0, templates - own)).reshape(templates, 1)
    vmem = pl.BlockSpec(memory_space=pltpu.VMEM)

    def kernel(*refs):
        search_kernel(block_rows, templates, *refs)

    out = pl.pallas_call(
        kernel,
        out_shape=jax.ShapeDtypeStruct((block_rows * templates, LANES), jnp.float32),
        in_specs=[pl.BlockSpec(memory_space=pltpu.SMEM), vmem, vmem, vmem],
        out_specs=vmem,
        scratch_shapes=[
            pltpu.VMEM((2, total_rows + 16, LANES), jnp.float32),
            pltpu.VMEM((window_rows, 4 * LANES), jnp.bfloat16),
            pltpu.VMEM((templates, 4 * LANES, 2 * LANES), jnp.bfloat16),
            pltpu.VMEM((window_rows * templates, LANES), jnp.float32),
        ],
        compiler_params=pltpu.CompilerParams(vmem_limit_bytes=56 * 1024 * 1024),
        name="search",
    )(harm_map[:, 0, :], index, bank.reshape(n_bank, 2 * LANES), normed_rows)
    out = out.reshape(block_rows, templates, LANES).transpose(1, 0, 2)
    return out.reshape(templates, block_rows * LANES)[:own]


def body(spectrum, bank, fdot_index, harm_map):
    block_len = spectrum.shape[1]
    bin_devices = lax.axis_size("bins")
    position = lax.axis_index("bins")
    total_bins = block_len * bin_devices
    first_bin = spectrum[:, :1]
    next_first = from_behind(first_bin, "bins", -1)
    partner, partner_first = (spectrum, next_first)
    for bit_number in range(bin_devices.bit_length() - 1):
        partner, partner_first = from_partner((partner, partner_first), "bins", bit_number)
    mirrored = jnp.concatenate([partner_first, partner[:, :0:-1]], axis=1)
    positions = position * block_len + jnp.arange(block_len, dtype=jnp.int32)
    out_real, out_imag = unpack(spectrum, mirrored, positions, total_bins)
    local_power = jnp.sum(out_real * out_real + out_imag * out_imag)
    total_power = lax.psum(local_power, "bins")
    scaling = lax.rsqrt(total_power / total_bins + 1e-06)
    normed = jnp.stack([out_real * scaling, out_imag * scaling]).astype(jnp.bfloat16)
    whole_spectrum = lax.all_gather(normed, "bins", axis=1, tiled=True)
    rows = whole_spectrum.reshape(2, total_bins // LANES, LANES)
    return search(rows, bank, fdot_index, harm_map, block_len // LANES)


def solution(mesh):
    placed = (P(None, ("groups", "bins")), P(), P("fdot"), P(None, "bins", None))
    return jax.shard_map(
        body, mesh=mesh, in_specs=placed, out_specs=P("fdot", ("groups", "bins")), check_vma=False
    )
```

profile of v0, /device:TPU:0, one launch (start us, length us, event | category | flops | bytes accessed | tf_op | source)
XLA Modules:
  0.0 114.4 jit_solution(148752739294891389)
XLA Ops:
  0.0 3.1 %collective-permute-start.3 = (f32[2,32768]{1,0:T(2,128)}, f32[2,32768]{1,0:T(2,128)S(1)}, u32[]{:S(2)}, u32[]{:S(2)}) collective-permute-start(f32[2,32768]{1,0:T(2,128)} %param.4), channel_id=1, source_target_pairs={{0,4},{4,0},{8,12},{12,8},{1,5},{5,1},{9,13},{13,9},{2,6},{6,2},{1... | collective-permute-start | bytes 786440 | tf_op jit(solution)/shard_map/ppermute | solution.py:23
  3.1 6.5 %collective-permute-done.3 = f32[2,32768]{1,0:T(2,128)S(1)} collective-permute-done((f32[2,32768]{1,0:T(2,128)}, f32[2,32768]{1,0:T(2,128)S(1)}, u32[]{:S(2)}, u32[]{:S(2)}) %collective-permute-start.3) | collective-permute-done | bytes 262176 | tf_op jit(solution)/shard_map/ppermute | solution.py:23
  9.6 2.8 %collective-permute-start.4 = (f32[2,32768]{1,0:T(2,128)S(1)}, f32[2,32768]{1,0:T(2,128)S(1)}, u32[]{:S(2)}, u32[]{:S(2)}) collective-permute-start(f32[2,32768]{1,0:T(2,128)S(1)} %collective-permute-done.3), channel_id=1, source_target_pairs={{0,8},{4,12},{8,0},{12,4},{1,9},{5,13},{9,1},{13,5},{2,10},{6,14},... | collective-permute-start | bytes 786440 | tf_op jit(solution)/shard_map/ppermute | solution.py:23
  12.3 0.7 slice.19
  13.0 1.3 %collective-permute-start = (f32[2,1]{1,0:T(2,128)S(1)}, f32[2,1]{1,0:T(2,128)S(1)}, u32[]{:S(2)}, u32[]{:S(2)}) collective-permute-start(f32[2,1]{1,0:T(2,128)S(1)} %slice.19), channel_id=1, source_target_pairs={{0,12},{4,0},{8,4},{12,8},{1,13},{5,1},{9,5},{13,9},{2,14},{6,2},{... | collective-permute-start | bytes 32 | tf_op jit(solution)/shard_map/ppermute | solution.py:17
  14.4 0.0 copy-start.3
  14.4 0.7 copy-done.3
  15.0 0.0 copy-start.2
  15.0 0.7 copy.6.refs_1_
  15.7 0.0 copy-done.2
  15.7 0.7 copy.5.refs_0_
  16.4 0.8 collective-permute-done
  17.1 7.0 %collective-permute-start.1 = (f32[2,1]{1,0:T(2,128)S(1)}, f32[2,1]{1,0:T(2,128)S(1)}, u32[]{:S(2)}, u32[]{:S(2)}) collective-permute-start(f32[2,1]{1,0:T(2,128)S(1)} %collective-permute-done), channel_id=1, source_target_pairs={{0,4},{4,0},{8,12},{12,8},{1,5},{5,1},{9,13},{13,9},{2,6},{6,2},{1... | collective-permute-start | bytes 32 | tf_op jit(solution)/shard_map/ppermute | solution.py:23
  24.1 1.6 %collective-permute-done.1 = f32[2,1]{1,0:T(2,128)S(1)} collective-permute-done((f32[2,1]{1,0:T(2,128)S(1)}, f32[2,1]{1,0:T(2,128)S(1)}, u32[]{:S(2)}, u32[]{:S(2)}) %collective-permute-start.1) | collective-permute-done | bytes 40 | tf_op jit(solution)/shard_map/ppermute | solution.py:23
  25.7 1.0 collective-permute-start.2
  26.7 0.0 collective-permute-done.4
  26.7 0.3 slice.24
  27.1 22.3 %reverse = f32[2,32768]{1,0:T(2,128)S(1)} reverse(f32[2,32768]{1,0:T(2,128)S(1)} %bitcast.26), dimensions={1} | reverse | bytes 524288
  49.3 0.0 copy-start
  49.3 0.3 slice.37
  49.6 0.0 collective-permute-done.2
  49.7 0.6 copy-done
  50.3 0.6 add_multiply_fusion.1
  50.9 0.2 subtract_multiply_fusion.1
  51.1 0.0 copy-start.1
  51.1 1.1 add_reduce_fusion
  52.2 0.0 copy-done.1
  52.2 0.6 copy.12
  52.8 12.3 %psum.7 = f32[]{:T(128)} all-reduce(f32[]{:T(128)} %add_reduce_fusion), channel_id=1, replica_groups=mesh['groups'=2,'bins'=4,'fdot'=4] {'bins'}, use_global_device_ids=true, to_apply=%region_1.0 | all-reduce | flops 1 | bytes 8 | tf_op jit(solution)/shard_map/psum | solution.py:199
  65.9 4.4 %multiply_convert_fusion.1 = (bf16[1,32768]{1,0:T(2,128)(2,1)S(1)}, bf16[1,32768]{1,0:T(2,128)(2,1)S(1)}) fusion(f32[1,32768]{1,0:T(1,128)S(1)} %subtract_multiply_fusion.1, f32[1,32768]{1,0:T(1,128)S(1)} %get-tuple-element.5, f32[1,32768]{1,0:T(1,128)S(1)} %get-tuple-element.8, f32[]{:T(128)S(6)} %rsqrt.3, s32[]{:T(128)S(6)} %mul.97, ...), kind=kLoop, calls=%fused_computation.7 | loop fusion | flops 491520 | bytes 655368 | tf_op jit(solution)/shard_map/convert
  70.2 0.3 pad_maximum_fusion.1
  70.5 15.7 %all_gather.3 = bf16[2,131072]{1,0:T(2,128)(2,1)S(1)} all-gather(bf16[2,32768]{1,0:T(2,128)(2,1)S(1)} %pad_maximum_fusion.1), channel_id=1, replica_groups=mesh['groups'=2,'bins'=4,'fdot'=4] {'bins'}, dimensions={1}, use_global_device_ids=true | all-gather | bytes 655360 | tf_op jit(solution)/shard_map/all_gather | solution.py:202
  86.3 0.9 copy.11
  87.1 27.3 %search.1 = f32[2048,128]{1,0:T(8,128)} custom-call(s32[7,4]{1,0:T(8,128)} %copy.5.refs_0_, s32[8,1]{1,0:T(8,128)} %copy.6.refs_1_, bf16[128,256]{1,0:T(8,128)(2,1)} %bitcast.27, bf16[2,1024,128]{2,1,0:T(8,128)(2,1)} %bitcast.20), custom_call_target="tpu_custom_call" | custom-call | tf_op jit(solution)/shard_map/search/pallas_call | solution.py:167
Async XLA Ops:
  0.0 9.6 %collective-permute-start.3 = (f32[2,32768]{1,0:T(2,128)}, f32[2,32768]{1,0:T(2,128)S(1)}, u32[]{:S(2)}, u32[]{:S(2)}) collective-permute-start(f32[2,32768]{1,0:T(2,128)} %param.4), channel_id=1, source_target_pairs={{0,4},{4,0},{8,12},{12,8},{1,5},{5,1},{9,13},{13,9},{2,6},{6,2},{1... | collective-permute-start | bytes 786440 | tf_op jit(solution)/shard_map/ppermute | solution.py:23
  9.6 17.1 %collective-permute-start.4 = (f32[2,32768]{1,0:T(2,128)S(1)}, f32[2,32768]{1,0:T(2,128)S(1)}, u32[]{:S(2)}, u32[]{:S(2)}) collective-permute-start(f32[2,32768]{1,0:T(2,128)S(1)} %collective-permute-done.3), channel_id=1, source_target_pairs={{0,8},{4,12},{8,0},{12,4},{1,9},{5,13},{9,1},{13,5},{2,10},{6,14},... | collective-permute-start | bytes 786440 | tf_op jit(solution)/shard_map/ppermute | solution.py:23
  13.0 4.1 %collective-permute-start = (f32[2,1]{1,0:T(2,128)S(1)}, f32[2,1]{1,0:T(2,128)S(1)}, u32[]{:S(2)}, u32[]{:S(2)}) collective-permute-start(f32[2,1]{1,0:T(2,128)S(1)} %slice.19), channel_id=1, source_target_pairs={{0,12},{4,0},{8,4},{12,8},{1,13},{5,1},{9,5},{13,9},{2,14},{6,2},{... | collective-permute-start | bytes 32 | tf_op jit(solution)/shard_map/ppermute | solution.py:17
  14.4 0.7 copy-start.3
  15.0 0.7 copy-start.2
  17.1 8.6 %collective-permute-start.1 = (f32[2,1]{1,0:T(2,128)S(1)}, f32[2,1]{1,0:T(2,128)S(1)}, u32[]{:S(2)}, u32[]{:S(2)}) collective-permute-start(f32[2,1]{1,0:T(2,128)S(1)} %collective-permute-done), channel_id=1, source_target_pairs={{0,4},{4,0},{8,12},{12,8},{1,5},{5,1},{9,13},{13,9},{2,6},{6,2},{1... | collective-permute-start | bytes 32 | tf_op jit(solution)/shard_map/ppermute | solution.py:23
  25.7 24.0 %collective-permute-start.2 = (f32[2,1]{1,0:T(2,128)S(1)}, f32[2,1]{1,0:T(2,128)S(1)}, u32[]{:S(2)}, u32[]{:S(2)}) collective-permute-start(f32[2,1]{1,0:T(2,128)S(1)} %collective-permute-done.1), channel_id=1, source_target_pairs={{0,8},{4,12},{8,0},{12,4},{1,9},{5,13},{9,1},{13,5},{2,10},{6,14},... | collective-permute-start | bytes 32 | tf_op jit(solution)/shard_map/ppermute | solution.py:23
  49.3 1.0 copy-start
  51.1 1.1 %copy-start.1 = (bf16[128,2,128]{2,1,0:T(2,128)(2,1)S(1)}, bf16[128,2,128]{2,1,0:T(2,128)(2,1)}, u32[]{:S(2)}) copy-start(bf16[128,2,128]{2,1,0:T(2,128)(2,1)} %param.5) | copy-start | bytes 196612
where the time goes:
time: 115 us; the launch traced here: 114 us
  blocking collectives  28 us (24%)
  local copies, waits for them, and re-layouts  27.7 us (24%)
  Pallas kernels  27.3 us (24%)
  starting transfers between devices  15.2 us (13%)
  waiting for transfers between devices  8.83 us (8%)
  other arithmetic  6.6 us (6%)
    pallas_call x1, Pallas kernels, search(): pl.pallas_call(kernel, out_shape=jax.ShapeDtypeStruct((block_rows * templ...  27.3 us
    unnamed x12, local copies, waits for them, and re-layouts  25.3 us
    all_gather x1, blocking collectives, body(): whole_spectrum = lax.all_gather(normed, 'bins', axis=1, tiled=True)  15.7 us
    ppermute x4, starting transfers between devices, from_partner(): return lax.ppermute(value, axis, pairs)  13.9 us
    psum x1, blocking collectives, body(): total_power = lax.psum(local_power, 'bins')  12.3 us
    ppermute x4, waiting for transfers between devices, from_partner(): return lax.ppermute(value, axis, pairs)  8.07 us
    another operation x1, other arithmetic  4.38 us
  transfers between devices with their start and end apart: 5, of which 3 were waited for; matrix products, arithmetic and copies ran while one was open for 22% of the time, Pallas kernels for 0%

commit v1 on v0

--- a/solution.py
+++ b/solution.py
@@ -11,31 +11,182 @@
 STRIDE_TABLE = (4, 2, 6, 1, 3, 5, 7)
 
 
-def from_behind(value, axis, steps):
-    count = lax.axis_size(axis)
-    pairs = [(source, (source + steps) % count) for source in range(count)]
-    return lax.ppermute(value, axis, pairs)
-
-
-def from_partner(value, axis, apart):
-    mask = 2**apart
-    pairs = [(source, source ^ mask) for source in range(lax.axis_size(axis))]
-    return lax.ppermute(value, axis, pairs)
-
-
-def unpack(packed, mirrored, positions, total_bins):
-    real_a, imag_a = (packed[0], packed[1])
-    real_b, imag_b = (mirrored[0], mirrored[1])
+def spread_kernel(bins, spec_ref, out_ref, mirror_ref, tiles_ref, trade_send, trade_recv,
+                  tile_send, tile_recv, part_send, part_recv, mate_send, mate_recv):
+    mesh_ids = pl.DeviceIdType.MESH
+    block_rows = spec_ref.shape[0] // 2
+    half = block_rows // 2
+    place = lax.axis_index("bins")
+    member = lax.axis_index("fdot")
+    side = lax.rem(member, 2)
+    mate = member + 1 - 2 * side
+    partner = bins - 1 - place
+    total_bins = bins * block_rows * LANES
+    lane = lax.broadcasted_iota(jnp.int32, (half, LANES), 1)
+    line = lax.broadcasted_iota(jnp.int32, (half, LANES), 0)
+
+    power = jnp.zeros((8, LANES), jnp.float32)
+    for first in range(0, 2 * block_rows, 64):
+        chunk = spec_ref[first : first + 64, :]
+        square = chunk * chunk
+        if first == 0:
+            row8 = lax.broadcasted_iota(jnp.int32, (64, LANES), 0)
+            lane8 = lax.broadcasted_iota(jnp.int32, (64, LANES), 1)
+            both = chunk[0:1, :] + chunk[1:2, :]
+            is_first = (lane8 == 0) & (place == 0)
+            square = jnp.where(is_first & (row8 == 0), both * both, square)
+            square = jnp.where(is_first & (row8 == 1), 0.0, square)
+        power = power + jnp.sum(square.reshape(8, 8, LANES), axis=0)
+    tiles_ref[place, :8, :] = power
+    tiles_ref[place, 8:, :] = spec_ref[:8, :]
+    mirror_ref[2 * half + 8 :, :] = jnp.zeros((8, LANES), jnp.float32)
+
+    barrier = pltpu.get_barrier_semaphore()
+    for step in range(1, bins):
+        pl.semaphore_signal(
+            barrier, inc=1, device_id={"bins": lax.rem(place + step, bins)}, device_id_type=mesh_ids
+        )
+    pl.semaphore_signal(barrier, inc=1, device_id={"fdot": mate}, device_id_type=mesh_ids)
+    pl.semaphore_wait(barrier, bins)
+
+    start = pl.multiple_of((1 - side) * (2 * half - 8), 8)
+    trade = pltpu.make_async_remote_copy(
+        src_ref=spec_ref.at[pl.ds(start, 2 * half + 8), :],
+        dst_ref=mirror_ref.at[pl.ds(0, 2 * half + 8), :],
+        send_sem=trade_send,
+        recv_sem=trade_recv,
+        device_id={"bins": partner},
+        device_id_type=mesh_ids,
+    )
+    tile_copies = []
+    for step in range(1, bins):
+        tile_copies.append(
+            pltpu.make_async_remote_copy(
+                src_ref=tiles_ref.at[place],
+                dst_ref=tiles_ref.at[place],
+                send_sem=tile_send.at[step],
+                recv_sem=tile_recv.at[step],
+                device_id={"bins": lax.rem(place + step, bins)},
+                device_id_type=mesh_ids,
+            )
+        )
+    for copy in tile_copies:
+        copy.start()
+    trade.start()
+
+    position = place * (block_rows * LANES) + (side * half + line) * LANES + lane
+    angle = position.astype(jnp.float32) * jnp.float32(math.pi / total_bins)
+    cosine = jnp.cos(angle)
+    sine = jnp.sin(angle)
+
+    for step in range(1, bins):
+        source = lax.rem(place + bins - step, bins)
+        pltpu.make_async_remote_copy(
+            src_ref=tiles_ref.at[source],
+            dst_ref=tiles_ref.at[source],
+            send_sem=tile_send.at[step],
+            recv_sem=tile_recv.at[step],
+            device_id={"bins": lax.rem(place + step, bins)},
+            device_id_type=mesh_ids,
+        ).wait_recv()
+    power = tiles_ref[0, :8, :]
+    for other in range(1, bins):
+        power = power + tiles_ref[other, :8, :]
+    total = jnp.sum(jnp.sum(power, axis=0, keepdims=True), axis=1, keepdims=True)
+    scaling = lax.rsqrt(total / total_bins + 1e-06)
+    after = tiles_ref[lax.rem(bins - place, bins), 8:, :]
+
+    trade.wait_recv()
+    own = pl.multiple_of(side * 2 * half, 8)
+    base = pl.multiple_of((1 - side) * 8, 8)
+    turn = (LANES - lane[:8]) & (LANES - 1)
+    flip = 7 - line[:8]
+    at_last = (line == half - 1) & (side == 0)
+    mirrored = []
+    for part in range(2):
+        here = mirror_ref[pl.ds(base + part, half, stride=2), :]
+        follow = mirror_ref[pl.ds(base + part + 2, half, stride=2), :]
+        follow = jnp.where(at_last, after[part : part + 1, :], follow)
+        groups = []
+        for first in range(half - 8, -1, -8):
+            piece = jnp.take_along_axis(here[first : first + 8, :], turn, axis=1)
+            piece = jnp.where(lane[:8] == 0, follow[first : first + 8, :], piece)
+            groups.append(jnp.take_along_axis(piece, flip, axis=0))
+        mirrored.append(jnp.concatenate(groups, axis=0))
+    real_a = spec_ref[pl.ds(own, half, stride=2), :]
+    imag_a = spec_ref[pl.ds(own + 1, half, stride=2), :]
+    real_b, imag_b = mirrored
     even_real = 0.5 * (real_a + real_b)
     even_imag = 0.5 * (imag_a - imag_b)
     odd_real = 0.5 * (imag_a + imag_b)
     odd_imag = 0.5 * (real_b - real_a)
-    angle = positions.astype(jnp.float32) * jnp.float32(math.pi / total_bins)
-    cosine = jnp.cos(angle)
-    sine = jnp.sin(angle)
     out_real = even_real + cosine * odd_real + sine * odd_imag
     out_imag = even_imag + cosine * odd_imag - sine * odd_real
-    return (out_real, out_imag)
+    mine = place * 2 + side
+    out_ref[mine, 0] = (out_real * scaling).astype(jnp.bfloat16)
+    out_ref[mine, 1] = (out_imag * scaling).astype(jnp.bfloat16)
+
+    def to_bins(slot, step):
+        return pltpu.make_async_remote_copy(
+            src_ref=out_ref.at[slot],
+            dst_ref=out_ref.at[slot],
+            send_sem=part_send.at[step],
+            recv_sem=part_recv.at[step],
+            device_id={"bins": lax.rem(place + step, bins)},
+            device_id_type=mesh_ids,
+        )
+
+    def to_mate(slot, step):
+        return pltpu.make_async_remote_copy(
+            src_ref=out_ref.at[slot],
+            dst_ref=out_ref.at[slot],
+            send_sem=mate_send.at[step],
+            recv_sem=mate_recv.at[step],
+            device_id={"fdot": mate},
+            device_id_type=mesh_ids,
+        )
+
+    sends = [to_bins(mine, step) for step in range(1, bins)] + [to_mate(mine, 0)]
+    for copy in sends:
+        copy.start()
+    for step in range(1, bins):
+        slot = lax.rem(place + bins - step, bins) * 2 + side
+        to_bins(slot, step).wait_recv()
+        copy = to_mate(slot, step)
+        copy.start()
+        sends.append(copy)
+    for step in range(bins):
+        slot = lax.rem(place + bins - step, bins) * 2 + 1 - side
+        to_mate(slot, step).wait_recv()
+    trade.wait_send()
+    for copy in tile_copies + sends:
+        copy.wait_send()
+
+
+def spread(spectrum):
+    bins = lax.axis_size("bins")
+    block_rows = spectrum.shape[1] // LANES
+    half = block_rows // 2
+    lines = spectrum.reshape(2, block_rows, LANES).transpose(1, 0, 2).reshape(2 * block_rows, LANES)
+    vmem = pl.BlockSpec(memory_space=pltpu.VMEM)
+
+    def kernel(*refs):
+        spread_kernel(bins, *refs)
+
+    dma = pltpu.SemaphoreType.DMA
+    return pl.pallas_call(
+        kernel,
+        out_shape=jax.ShapeDtypeStruct((2 * bins, 2, half, LANES), jnp.bfloat16),
+        in_specs=[vmem],
+        out_specs=vmem,
+        scratch_shapes=[
+            pltpu.VMEM((2 * half + 16, LANES), jnp.float32),
+            pltpu.VMEM((bins, 16, LANES), jnp.float32),
+            dma, dma, dma((bins,)), dma((bins,)), dma((bins,)), dma((bins,)), dma((bins,)), dma((bins,)),
+        ],
+        compiler_params=pltpu.CompilerParams(collective_id=0, has_side_effects=True),
+        name="spread",
+    )(lines)
 
 
 def search_layout(block_rows):
@@ -51,7 +202,8 @@
 def search_kernel(block_rows, templates, harm_ref, index_ref, bank_ref, spec_ref, out_ref,
                   lines_ref, window_ref, weight_ref, plane_ref):
     spans, window_rows = search_layout(block_rows)
-    total_rows = spec_ref.shape[1]
+    half = spec_ref.shape[2]
+    total_rows = spec_ref.shape[0] * half
     position = lax.axis_index("bins")
     n_bank = bank_ref.shape[0]
     lane_of = lax.broadcasted_iota(jnp.int32, (templates, n_bank), 1)
@@ -80,12 +232,10 @@
         lines_ref[part, :8, :] = jnp.zeros((8, LANES), jnp.float32)
         lines_ref[part, pl.ds(8 + total_rows, 8), :] = jnp.zeros((8, LANES), jnp.float32)
 
-        @pl.loop(0, total_rows // 256)
+        @pl.loop(0, spec_ref.shape[0])
         def _(step, part=part):
-            row = pl.multiple_of(step * 256, 256)
-            lines_ref[part, pl.ds(row + 8, 256), :] = spec_ref[part, pl.ds(row, 256), :].astype(
-                jnp.float32
-            )
+            row = pl.multiple_of(step * half, half)
+            lines_ref[part, pl.ds(row + 8, half), :] = spec_ref[step, part].astype(jnp.float32)
 
     for stride, first, count in spans:
         start = position * (stride * block_rows // 8)
@@ -152,11 +302,11 @@
             out_ref[pl.ds(row, templates), :] = sums[unit] * 0.125
 
 
-def search(normed_rows, bank, fdot_index, harm_map, block_rows):
+def search(pieces, bank, fdot_index, harm_map, block_rows):
     own = fdot_index.shape[0]
     templates = -(-own // 8) * 8
     n_bank = bank.shape[0]
-    total_rows = normed_rows.shape[1]
+    total_rows = pieces.shape[0] * pieces.shape[2]
     spans, window_rows = search_layout(block_rows)
     index = jnp.pad(fdot_index, (0, templates - own)).reshape(templates, 1)
     vmem = pl.BlockSpec(memory_space=pltpu.VMEM)
@@ -177,31 +327,14 @@
         ],
         compiler_params=pltpu.CompilerParams(vmem_limit_bytes=56 * 1024 * 1024),
         name="search",
-    )(harm_map[:, 0, :], index, bank.reshape(n_bank, 2 * LANES), normed_rows)
+    )(harm_map[:, 0, :], index, bank.reshape(n_bank, 2 * LANES), pieces)
     out = out.reshape(block_rows, templates, LANES).transpose(1, 0, 2)
     return out.reshape(templates, block_rows * LANES)[:own]
 
 
 def body(spectrum, bank, fdot_index, harm_map):
-    block_len = spectrum.shape[1]
-    bin_devices = lax.axis_size("bins")
-    position = lax.axis_index("bins")
-    total_bins = block_len * bin_devices
-    first_bin = spectrum[:, :1]
-    next_first = from_behind(first_bin, "bins", -1)
-    partner, partner_first = (spectrum, next_first)
-    for bit_number in range(bin_devices.bit_length() - 1):
-        partner, partner_first = from_partner((partner, partner_first), "bins", bit_number)
-    mirrored = jnp.concatenate([partner_first, partner[:, :0:-1]], axis=1)
-    positions = position * block_len + jnp.arange(block_len, dtype=jnp.int32)
-    out_real, out_imag = unpack(spectrum, mirrored, positions, total_bins)
-    local_power = jnp.sum(out_real * out_real + out_imag * out_imag)
-    total_power = lax.psum(local_power, "bins")
-    scaling = lax.rsqrt(total_power / total_bins + 1e-06)
-    normed = jnp.stack([out_real * scaling, out_imag * scaling]).astype(jnp.bfloat16)
-    whole_spectrum = lax.all_gather(normed, "bins", axis=1, tiled=True)
-    rows = whole_spectrum.reshape(2, total_bins // LANES, LANES)
-    return search(rows, bank, fdot_index, harm_map, block_len // LANES)
+    pieces = spread(spectrum)
+    return search(pieces, bank, fdot_index, harm_map, spectrum.shape[1] // LANES)
 
 
 def solution(mesh):

time: 115 us -> 51.7 us (0.45)
  blocking collectives: 28 us -> 0 us
  local copies, waits for them, and re-layouts: 27.7 us -> 3.47 us
  Pallas kernels: 27.3 us -> 48 us
  starting transfers between devices: 15.2 us -> 0 us
  waiting for transfers between devices: 8.83 us -> 0 us
  other arithmetic: 6.6 us -> 0 us
    unnamed x12 -> x5, local copies, waits for them, and re-layouts: 25.3 us -> 2.13 us
    pallas_call x0 -> x1, Pallas kernels: none -> 20.7 us  [spread(): pl.pallas_call(kernel, out_shape=jax.ShapeDtypeStruct((2 * bins, 2, half,...]
    all_gather x1 -> x0, blocking collectives: 15.7 us -> none  [body(): whole_spectrum = lax.all_gather(normed, 'bins', axis=1, tiled=True)]
    ppermute x5 -> x0, starting transfers between devices: 15.2 us -> none  [the longest x4 13.9 us: from_partner(): return lax.ppermute(value, axis, pairs)]
    psum x1 -> x0, blocking collectives: 12.3 us -> none  [body(): total_power = lax.psum(local_power, 'bins')]
    ppermute x5 -> x0, waiting for transfers between devices: 8.83 us -> none  [the longest x4 8.07 us: from_partner(): return lax.ppermute(value, axis, pairs)]
    another operation x2 -> x0, other arithmetic: 4.68 us -> none
  transfers between devices with their start and end apart: 5 -> 0, of which waited for: 3 -> 0; matrix products, arithmetic and copies ran while one was open for 22% -> 0% of each run, Pallas kernels for 0% -> 0%
where the time goes in v1:
time: 51.7 us; the launch traced here: 51.4 us
  Pallas kernels  48 us (93%)
  local copies, waits for them, and re-layouts  3.47 us (7%)
    pallas_call x1, Pallas kernels, search(): pl.pallas_call(kernel, out_shape=jax.ShapeDtypeStruct((block_rows * templ...  27.3 us
    pallas_call x1, Pallas kernels, spread(): pl.pallas_call(kernel, out_shape=jax.ShapeDtypeStruct((2 * bins, 2, half,...  20.7 us
    unnamed x5, local copies, waits for them, and re-layouts  2.13 us

profile of v1, /device:TPU:0, one launch (start us, length us, event | category | flops | bytes accessed | tf_op | source)
XLA Modules:
  0.0 51.4 jit_solution(6522980251659227960)
XLA Ops:
  0.0 0.0 copy-start.1
  0.0 0.7 %copy-done.1 = s32[8]{0:T(128)S(1)} copy-done((s32[8]{0:T(128)S(1)}, s32[8]{0:T(128)}, u32[]{:S(2)}) %copy-start.1) | copy-done | bytes 56
  0.7 0.0 copy-start
  0.7 0.7 %copy.7.refs_1_ = s32[8,1]{1,0:T(8,128)} copy(s32[8,1]{0,1:T(1,128)S(1)} %bitcast.20) | data formatting | bytes 64 | tf_op jit(solution)/shard_map/reshape | solution.py:311
  1.3 0.0 copy-done
  1.3 0.7 %copy.6.refs_0_ = s32[7,4]{1,0:T(8,128)} copy(s32[7,4]{0,1:T(4,128)S(1)} %bitcast.19) | data formatting | bytes 224 | tf_op jit(solution)/shard_map/squeeze | solution.py:330
  2.0 1.5 %copy.10 = bf16[16,8,2,128]{3,1,2,0:T(8,128)(2,1)} copy(bf16[16,8,2,128]{3,2,1,0:T(2,128)(2,1)} %bitcast.18) | data formatting | bytes 131072
  3.5 20.7 %spread.1.refs_3_ = bf16[8,2,128,128]{3,2,1,0:T(8,128)(2,1)} custom-call(f32[512,128]{1,0:T(8,128)} %bitcast.16), custom_call_target="tpu_custom_call" | custom-call | tf_op jit(solution)/shard_map/spread/pallas_call | solution.py:177
  24.2 27.3 %search.1 = f32[2048,128]{1,0:T(8,128)} custom-call(s32[7,4]{1,0:T(8,128)} %copy.6.refs_0_, s32[8,1]{1,0:T(8,128)} %copy.7.refs_1_, bf16[128,256]{1,0:T(8,128)(2,1)} %bitcast.17, bf16[8,2,128,128]{3,2,1,0:T(8,128)(2,1)} %spread.1.refs_3_), custom_call_target="tpu_custom_call" | custom-call | tf_op jit(solution)/shard_map/search/pallas_call | solution.py:317
Async XLA Ops:
  0.0 0.7 %copy-start.1 = (s32[8]{0:T(128)S(1)}, s32[8]{0:T(128)}, u32[]{:S(2)}) copy-start(s32[8]{0:T(128)} %param.6) | copy-start | bytes 100
  0.7 0.7 %copy-start = (s32[7,1,4]{0,2,1:T(4,128)S(1)}, s32[7,1,4]{0,2,1:T(4,128)}, u32[]{:S(2)}) copy-start(s32[7,1,4]{0,2,1:T(4,128)} %param.7) | copy-start | bytes 340

commit v2 on v1

--- a/solution.py
+++ b/solution.py
@@ -196,30 +196,33 @@
         count = stride * block_rows // 8 + 16
         spans.append((stride, row, count))
         row += count
-    return spans, -(-row // 256) * 256
+    return spans, row
 
 
 def search_kernel(block_rows, templates, harm_ref, index_ref, bank_ref, spec_ref, out_ref,
                   lines_ref, window_ref, weight_ref, plane_ref):
-    spans, window_rows = search_layout(block_rows)
+    spans, _ = search_layout(block_rows)
     half = spec_ref.shape[2]
     total_rows = spec_ref.shape[0] * half
     position = lax.axis_index("bins")
-    n_bank = bank_ref.shape[0]
-    lane_of = lax.broadcasted_iota(jnp.int32, (templates, n_bank), 1)
-    onehot = jnp.where(index_ref[...] == lane_of, 1.0, 0.0).astype(jnp.bfloat16)
+    bank_rows = bank_ref.shape[0]
+    lane_of = lax.broadcasted_iota(jnp.int32, (2 * templates, bank_rows), 1)
+    line_of = lax.broadcasted_iota(jnp.int32, (2 * templates, bank_rows), 0)
+    chosen = jnp.zeros((2 * templates, bank_rows), jnp.int32)
+    for template in range(index_ref.shape[0]):
+        chosen = jnp.where(line_of == template, 2 * index_ref[template], chosen)
+        chosen = jnp.where(line_of == templates + template, 2 * index_ref[template] + 1, chosen)
+    onehot = jnp.where(chosen == lane_of, 1.0, 0.0).astype(jnp.bfloat16)
     taps = jnp.dot(onehot, bank_ref[...], preferred_element_type=jnp.float32).astype(jnp.bfloat16)
     tap = lax.broadcasted_iota(jnp.int32, (LANES, 2 * LANES), 0)
     lane = lax.broadcasted_iota(jnp.int32, (LANES, 2 * LANES), 1)
     turn = jnp.where((tap + lane) % (2 * LANES) == 0, 1.0, 0.0).astype(jnp.bfloat16)
-    turned = [
-        jnp.dot(taps[:, part * LANES : (part + 1) * LANES], turn, preferred_element_type=jnp.float32)
-        for part in range(2)
-    ]
+    turned = jnp.dot(taps, turn, preferred_element_type=jnp.float32)
     for template in range(templates):
         parts = []
         for part in range(2):
-            row = jnp.broadcast_to(turned[part][template : template + 1, :], (2 * LANES, 2 * LANES))
+            line = part * templates + template
+            row = jnp.broadcast_to(turned[line : line + 1, :], (2 * LANES, 2 * LANES))
             rolled = pltpu.roll(row, 0, 1, stride=1, stride_axis=0)
             parts.append(rolled[:, :LANES].astype(jnp.bfloat16))
         real, imag = parts
@@ -227,79 +230,79 @@
         weight_ref[template, : 2 * LANES, LANES:] = imag
         weight_ref[template, 2 * LANES :, :LANES] = -imag
         weight_ref[template, 2 * LANES :, LANES:] = real
-    low_half = lax.broadcasted_iota(jnp.int32, (1, LANES), 1) < LANES // 2
     for part in range(2):
         lines_ref[part, :8, :] = jnp.zeros((8, LANES), jnp.float32)
         lines_ref[part, pl.ds(8 + total_rows, 8), :] = jnp.zeros((8, LANES), jnp.float32)
 
-        @pl.loop(0, spec_ref.shape[0])
-        def _(step, part=part):
-            row = pl.multiple_of(step * half, half)
-            lines_ref[part, pl.ds(row + 8, half), :] = spec_ref[step, part].astype(jnp.float32)
-
-    for stride, first, count in spans:
-        start = position * (stride * block_rows // 8)
-        piece = 16
+    @pl.loop(0, spec_ref.shape[0])
+    def _(step):
+        row = pl.multiple_of(step * half, half)
         for part in range(2):
-
-            @pl.loop(0, count // piece)
-            def _(step, part=part, first=first, start=start):
-                row = pl.multiple_of(step * piece, piece)
-                source = pl.multiple_of(start + row, 8)
-                before = pltpu.roll(lines_ref[part, pl.ds(source + 7, piece), :], LANES // 2, 1)
-                here = pltpu.roll(lines_ref[part, pl.ds(source + 8, piece), :], LANES // 2, 1)
-                after = pltpu.roll(lines_ref[part, pl.ds(source + 9, piece), :], LANES // 2, 1)
-                target = pl.ds(pl.multiple_of(first + row, piece), piece)
-                window_ref[target, pl.ds(2 * part * LANES, LANES)] = jnp.where(
-                    low_half, before, here
-                ).astype(jnp.bfloat16)
-                window_ref[target, pl.ds((2 * part + 1) * LANES, LANES)] = jnp.where(
-                    low_half, here, after
-                ).astype(jnp.bfloat16)
-
-    used = spans[-1][1] + spans[-1][2]
-    if used < window_rows:
-        window_ref[used:, :] = jnp.zeros((window_rows - used, 4 * LANES), jnp.bfloat16)
-
-    @pl.loop(0, window_rows // 256)
+            lines_ref[part, pl.ds(row + 8, half), :] = pltpu.roll(
+                spec_ref[step, part].astype(jnp.float32), LANES // 2, 1
+            )
+
+    low_half = lax.broadcasted_iota(jnp.int32, (half, LANES), 1) < LANES // 2
+
+    @pl.loop(0, spec_ref.shape[0])
     def _(step):
-        row = pl.multiple_of(step * 256, 256)
-        lhs = window_ref[pl.ds(row, 256), :]
-        for template in range(templates):
-            amps = jnp.dot(lhs, weight_ref[template], preferred_element_type=jnp.float32)
+        row = pl.multiple_of(step * half, half)
+        target = pl.ds(row, half)
+        for part in range(2):
+            before = lines_ref[part, pl.ds(row + 7, half), :]
+            here = lines_ref[part, pl.ds(row + 8, half), :]
+            after = lines_ref[part, pl.ds(row + 9, half), :]
+            window_ref[target, 2 * part * LANES : (2 * part + 1) * LANES] = jnp.where(
+                low_half, before, here
+            ).astype(jnp.bfloat16)
+            window_ref[target, (2 * part + 1) * LANES : (2 * part + 2) * LANES] = jnp.where(
+                low_half, here, after
+            ).astype(jnp.bfloat16)
+
+    @pl.loop(0, templates)
+    def _(template):
+        weight = weight_ref[template]
+        for stride, first, count in spans:
+            start = pl.multiple_of(position * (stride * block_rows // 8), 16)
+            amps = jnp.dot(
+                window_ref[pl.ds(start, count), :], weight, preferred_element_type=jnp.float32
+            )
             real, imag = amps[:, :LANES], amps[:, LANES:]
-            plane_ref[pl.ds(row * templates + template, 256, stride=templates), :] = (
+            plane_ref[pl.ds(first * templates + template, count, stride=templates), :] = (
                 real * real + imag * imag
             )
 
     column = lax.broadcasted_iota(jnp.int32, (templates, LANES), 1)
-
-    @pl.loop(0, block_rows // 8)
-    def _(group):
-        sums = []
+    wide = 8
+    bases = [
+        (column * stride + harm_ref[3, number]) >> 3 for number, stride in enumerate(STRIDE_TABLE)
+    ]
+
+    @pl.loop(0, block_rows // (8 * wide))
+    def _(block):
+        def rows_at(line):
+            row = pl.multiple_of(line * templates, templates)
+            return plane_ref[pl.ds(row, templates), :]
+
         for unit in range(8):
-            row = pl.multiple_of((group * 8 + unit) * templates, templates)
-            sums.append(plane_ref[pl.ds(row, templates), :])
-        for number, (stride, first, _) in enumerate(spans[1:]):
-            base = (column * stride + harm_ref[number, 3]) // 8
-
-            def source_row(line, first=first, stride=stride):
-                row = (first + group * stride + line) * templates
-                return plane_ref[pl.ds(pl.multiple_of(row, templates), templates), :]
-
-            for unit in range(8):
+            sums = [rows_at((block * wide + group) * 8 + unit) for group in range(wide)]
+            for number, (stride, first, _) in enumerate(spans[1:]):
                 begin = unit * stride * (LANES // 8)
                 line, offset = begin // LANES, begin % LANES
-                where = base + offset
+                where = bases[number] + offset
                 wrapped = where & (LANES - 1)
-                picked = jnp.take_along_axis(source_row(line), wrapped, axis=1)
-                if offset + stride * (LANES // 8) >= LANES:
-                    follow = jnp.take_along_axis(source_row(line + 1), wrapped, axis=1)
-                    picked = jnp.where(where < LANES, picked, follow)
-                sums[unit] = sums[unit] + picked
-        for unit in range(8):
-            row = pl.multiple_of((group * 8 + unit) * templates, templates)
-            out_ref[pl.ds(row, templates), :] = sums[unit] * 0.125
+                straddles = offset + stride * (LANES // 8) >= LANES
+                inside = where < LANES
+                for group in range(wide):
+                    source = first + (block * wide + group) * stride + line
+                    picked = jnp.take_along_axis(rows_at(source), wrapped, axis=1)
+                    if straddles:
+                        follow = jnp.take_along_axis(rows_at(source + 1), wrapped, axis=1)
+                        picked = jnp.where(inside, picked, follow)
+                    sums[group] = sums[group] + picked
+            for group in range(wide):
+                row = pl.multiple_of(((block * wide + group) * 8 + unit) * templates, templates)
+                out_ref[pl.ds(row, templates), :] = sums[group] * 0.125
 
 
 def search(pieces, bank, fdot_index, harm_map, block_rows):
@@ -307,9 +310,9 @@
     templates = -(-own // 8) * 8
     n_bank = bank.shape[0]
     total_rows = pieces.shape[0] * pieces.shape[2]
-    spans, window_rows = search_layout(block_rows)
-    index = jnp.pad(fdot_index, (0, templates - own)).reshape(templates, 1)
+    _, plane_rows = search_layout(block_rows)
     vmem = pl.BlockSpec(memory_space=pltpu.VMEM)
+    smem = pl.BlockSpec(memory_space=pltpu.SMEM)
 
     def kernel(*refs):
         search_kernel(block_rows, templates, *refs)
@@ -317,17 +320,17 @@
     out = pl.pallas_call(
         kernel,
         out_shape=jax.ShapeDtypeStruct((block_rows * templates, LANES), jnp.float32),
-        in_specs=[pl.BlockSpec(memory_space=pltpu.SMEM), vmem, vmem, vmem],
+        in_specs=[smem, smem, vmem, vmem],
         out_specs=vmem,
         scratch_shapes=[
             pltpu.VMEM((2, total_rows + 16, LANES), jnp.float32),
-            pltpu.VMEM((window_rows, 4 * LANES), jnp.bfloat16),
+            pltpu.VMEM((total_rows, 4 * LANES), jnp.bfloat16),
             pltpu.VMEM((templates, 4 * LANES, 2 * LANES), jnp.bfloat16),
-            pltpu.VMEM((window_rows * templates, LANES), jnp.float32),
+            pltpu.VMEM((plane_rows * templates, LANES), jnp.float32),
         ],
         compiler_params=pltpu.CompilerParams(vmem_limit_bytes=56 * 1024 * 1024),
         name="search",
-    )(harm_map[:, 0, :], index, bank.reshape(n_bank, 2 * LANES), pieces)
+    )(harm_map[:, 0, :].T, fdot_index, bank.reshape(2 * n_bank, LANES), pieces)
     out = out.reshape(block_rows, templates, LANES).transpose(1, 0, 2)
     return out.reshape(templates, block_rows * LANES)[:own]
 

time: 51.7 us -> 32.9 us (0.64)
  Pallas kernels: 48 us -> 32.7 us
  local copies, waits for them, and re-layouts: 3.47 us -> 0 us
    pallas_call x1, Pallas kernels: 27.3 us -> 12 us  [search(): pl.pallas_call(kernel, out_shape=jax.ShapeDtypeStruct((block_rows * templ...]
    unnamed x5 -> x0, local copies, waits for them, and re-layouts: 2.13 us -> none
    reshape x1 -> x0, local copies, waits for them, and re-layouts: 0.67 us -> none  [search(): index = jnp.pad(fdot_index, (0, templates - own)).reshape(templates, 1)]
    squeeze x1 -> x0, local copies, waits for them, and re-layouts: 0.66 us -> none  [search(): harm_map[:, 0, :]]
where the time goes in v2:
time: 32.9 us; the launch traced here: 32.7 us
  Pallas kernels  32.7 us (99%)
    pallas_call x1, Pallas kernels, spread(): pl.pallas_call(kernel, out_shape=jax.ShapeDtypeStruct((2 * bins, 2, half,...  20.7 us
    pallas_call x1, Pallas kernels, search(): pl.pallas_call(kernel, out_shape=jax.ShapeDtypeStruct((block_rows * templ...  12 us

profile of v2, /device:TPU:0, one launch (start us, length us, event | category | flops | bytes accessed | tf_op | source)
XLA Modules:
  0.0 32.7 jit_solution(1513352110106075892)
XLA Ops:
  0.0 20.7 %spread.1.refs_3_ = bf16[8,2,128,128]{3,2,1,0:T(8,128)(2,1)} custom-call(f32[512,128]{1,0:T(8,128)} %bitcast.14), custom_call_target="tpu_custom_call" | custom-call | tf_op jit(solution)/shard_map/spread/pallas_call | solution.py:177
  20.7 12.0 %search.1 = f32[2048,128]{1,0:T(8,128)} custom-call(s32[4,7]{1,0:T(4,128)} %bitcast.16, s32[8]{0:T(128)} %refs_1_.1, bf16[256,128]{1,0:T(8,128)(2,1)} %bitcast.15, bf16[8,2,128,128]{3,2,1,0:T(8,128)(2,1)} %spread.1.refs_3_), custom_call_target="tpu_custom_call" | custom-call | tf_op jit(solution)/shard_map/search/pallas_call | solution.py:320

commit v3 on v2

--- a/solution.py
+++ b/solution.py
@@ -11,19 +11,51 @@
 STRIDE_TABLE = (4, 2, 6, 1, 3, 5, 7)
 
 
+WAYS = 4
+
+
+def unpack(real_a, imag_a, real_b, imag_b, position, total_bins):
+    even_real = 0.5 * (real_a + real_b)
+    even_imag = 0.5 * (imag_a - imag_b)
+    odd_real = 0.5 * (imag_a + imag_b)
+    odd_imag = 0.5 * (real_b - real_a)
+    angle = position.astype(jnp.float32) * jnp.float32(math.pi / total_bins)
+    cosine = jnp.cos(angle)
+    sine = jnp.sin(angle)
+    out_real = even_real + cosine * odd_real + sine * odd_imag
+    out_imag = even_imag + cosine * odd_imag - sine * odd_real
+    return out_real, out_imag
+
+
+def mirror(here, follow):
+    lane = lax.broadcasted_iota(jnp.int32, (8, LANES), 1)
+    turn = (LANES - lane) & (LANES - 1)
+    flip = 7 - lax.broadcasted_iota(jnp.int32, (8, LANES), 0)
+    groups = []
+    for first in range(here.shape[0] - 8, -1, -8):
+        piece = jnp.take_along_axis(here[first : first + 8, :], turn, axis=1)
+        piece = jnp.where(lane == 0, follow[first : first + 8, :], piece)
+        groups.append(jnp.take_along_axis(piece, flip, axis=0))
+    return jnp.concatenate(groups, axis=0)
+
+
 def spread_kernel(bins, spec_ref, out_ref, mirror_ref, tiles_ref, trade_send, trade_recv,
-                  tile_send, tile_recv, part_send, part_recv, mate_send, mate_recv):
+                  tile_send, tile_recv, part_send, part_recv, side_send, side_recv,
+                  mate_send, mate_recv):
     mesh_ids = pl.DeviceIdType.MESH
     block_rows = spec_ref.shape[0] // 2
-    half = block_rows // 2
+    unit = block_rows // (2 * WAYS)
     place = lax.axis_index("bins")
-    member = lax.axis_index("fdot")
-    side = lax.rem(member, 2)
-    mate = member + 1 - 2 * side
+    whole_member = lax.axis_index("fdot")
+    member = lax.rem(whole_member, WAYS)
+    mate = whole_member + 1 - 2 * lax.rem(member, 2)
+    across = whole_member + 2 - 4 * (member // 2)
+    mate_member = member + 1 - 2 * lax.rem(member, 2)
+    across_member = member + 2 - 4 * (member // 2)
+    mate_across = mate_member + 2 - 4 * (mate_member // 2)
     partner = bins - 1 - place
     total_bins = bins * block_rows * LANES
-    lane = lax.broadcasted_iota(jnp.int32, (half, LANES), 1)
-    line = lax.broadcasted_iota(jnp.int32, (half, LANES), 0)
+    edge = jnp.where(member == 0, 1, 0)
 
     power = jnp.zeros((8, LANES), jnp.float32)
     for first in range(0, 2 * block_rows, 64):
@@ -39,125 +71,132 @@
         power = power + jnp.sum(square.reshape(8, 8, LANES), axis=0)
     tiles_ref[place, :8, :] = power
     tiles_ref[place, 8:, :] = spec_ref[:8, :]
-    mirror_ref[2 * half + 8 :, :] = jnp.zeros((8, LANES), jnp.float32)
+    mirror_ref[2 * unit + 8 :, :] = jnp.zeros((8, LANES), jnp.float32)
 
     barrier = pltpu.get_barrier_semaphore()
     for step in range(1, bins):
         pl.semaphore_signal(
             barrier, inc=1, device_id={"bins": lax.rem(place + step, bins)}, device_id_type=mesh_ids
         )
-    pl.semaphore_signal(barrier, inc=1, device_id={"fdot": mate}, device_id_type=mesh_ids)
-    pl.semaphore_wait(barrier, bins)
-
-    start = pl.multiple_of((1 - side) * (2 * half - 8), 8)
+    for other in (mate, across):
+        pl.semaphore_signal(barrier, inc=1, device_id={"fdot": other}, device_id_type=mesh_ids)
+    pl.semaphore_wait(barrier, bins + 1)
+
+    low = 2 * unit * member
+    high = block_rows - unit - low
+    start = pl.multiple_of(2 * high - 8 * edge, 8)
     trade = pltpu.make_async_remote_copy(
-        src_ref=spec_ref.at[pl.ds(start, 2 * half + 8), :],
-        dst_ref=mirror_ref.at[pl.ds(0, 2 * half + 8), :],
+        src_ref=spec_ref.at[pl.ds(start, 2 * unit + 8), :],
+        dst_ref=mirror_ref.at[pl.ds(0, 2 * unit + 8), :],
         send_sem=trade_send,
         recv_sem=trade_recv,
         device_id={"bins": partner},
         device_id_type=mesh_ids,
     )
-    tile_copies = []
-    for step in range(1, bins):
-        tile_copies.append(
-            pltpu.make_async_remote_copy(
-                src_ref=tiles_ref.at[place],
-                dst_ref=tiles_ref.at[place],
-                send_sem=tile_send.at[step],
-                recv_sem=tile_recv.at[step],
-                device_id={"bins": lax.rem(place + step, bins)},
-                device_id_type=mesh_ids,
-            )
-        )
-    for copy in tile_copies:
-        copy.start()
-    trade.start()
-
-    position = place * (block_rows * LANES) + (side * half + line) * LANES + lane
-    angle = position.astype(jnp.float32) * jnp.float32(math.pi / total_bins)
-    cosine = jnp.cos(angle)
-    sine = jnp.sin(angle)
-
-    for step in range(1, bins):
-        source = lax.rem(place + bins - step, bins)
-        pltpu.make_async_remote_copy(
-            src_ref=tiles_ref.at[source],
-            dst_ref=tiles_ref.at[source],
+
+    def tile_copy(slot, step):
+        return pltpu.make_async_remote_copy(
+            src_ref=tiles_ref.at[slot],
+            dst_ref=tiles_ref.at[slot],
             send_sem=tile_send.at[step],
             recv_sem=tile_recv.at[step],
             device_id={"bins": lax.rem(place + step, bins)},
             device_id_type=mesh_ids,
-        ).wait_recv()
+        )
+
+    def piece_copy(slot, step, send, recv, device):
+        return pltpu.make_async_remote_copy(
+            src_ref=out_ref.at[slot],
+            dst_ref=out_ref.at[slot],
+            send_sem=send.at[step],
+            recv_sem=recv.at[step],
+            device_id=device,
+            device_id_type=mesh_ids,
+        )
+
+    def to_bins(slot, step):
+        device = {"bins": lax.rem(place + step, bins)}
+        return piece_copy(slot, step, part_send, part_recv, device)
+
+    def to_across(slot, step):
+        return piece_copy(slot, step, side_send, side_recv, {"fdot": across})
+
+    def to_mate(slot, step):
+        return piece_copy(slot, step, mate_send, mate_recv, {"fdot": mate})
+
+    tile_copies = [tile_copy(place, step) for step in range(bins - 1, 0, -1)]
+    trade.start()
+    for copy in tile_copies:
+        copy.start()
+
+    lane = lax.broadcasted_iota(jnp.int32, (unit, LANES), 1)
+    line = lax.broadcasted_iota(jnp.int32, (unit, LANES), 0)
+    own_position = (place * block_rows + low + line) * LANES + lane
+    far_position = (partner * block_rows + high + line) * LANES + lane
+
+    for step in range(1, bins):
+        tile_copy(lax.rem(place + bins - step, bins), step).wait_recv()
     power = tiles_ref[0, :8, :]
     for other in range(1, bins):
         power = power + tiles_ref[other, :8, :]
     total = jnp.sum(jnp.sum(power, axis=0, keepdims=True), axis=1, keepdims=True)
     scaling = lax.rsqrt(total / total_bins + 1e-06)
     after = tiles_ref[lax.rem(bins - place, bins), 8:, :]
+    own_row = pl.multiple_of(2 * low, 8)
+    base = pl.multiple_of(8 * edge, 8)
+    own = [spec_ref[pl.ds(own_row + part, unit, stride=2), :] for part in range(2)]
+    own_follow = [spec_ref[pl.ds(own_row + part + 2, unit, stride=2), :] for part in range(2)]
+    own_mirror = [mirror(own[part], own_follow[part]) for part in range(2)]
+    at_last = (line == unit - 1) & (member == 0)
 
     trade.wait_recv()
-    own = pl.multiple_of(side * 2 * half, 8)
-    base = pl.multiple_of((1 - side) * 8, 8)
-    turn = (LANES - lane[:8]) & (LANES - 1)
-    flip = 7 - line[:8]
-    at_last = (line == half - 1) & (side == 0)
-    mirrored = []
-    for part in range(2):
-        here = mirror_ref[pl.ds(base + part, half, stride=2), :]
-        follow = mirror_ref[pl.ds(base + part + 2, half, stride=2), :]
-        follow = jnp.where(at_last, after[part : part + 1, :], follow)
-        groups = []
-        for first in range(half - 8, -1, -8):
-            piece = jnp.take_along_axis(here[first : first + 8, :], turn, axis=1)
-            piece = jnp.where(lane[:8] == 0, follow[first : first + 8, :], piece)
-            groups.append(jnp.take_along_axis(piece, flip, axis=0))
-        mirrored.append(jnp.concatenate(groups, axis=0))
-    real_a = spec_ref[pl.ds(own, half, stride=2), :]
-    imag_a = spec_ref[pl.ds(own + 1, half, stride=2), :]
-    real_b, imag_b = mirrored
-    even_real = 0.5 * (real_a + real_b)
-    even_imag = 0.5 * (imag_a - imag_b)
-    odd_real = 0.5 * (imag_a + imag_b)
-    odd_imag = 0.5 * (real_b - real_a)
-    out_real = even_real + cosine * odd_real + sine * odd_imag
-    out_imag = even_imag + cosine * odd_imag - sine * odd_real
-    mine = place * 2 + side
-    out_ref[mine, 0] = (out_real * scaling).astype(jnp.bfloat16)
-    out_ref[mine, 1] = (out_imag * scaling).astype(jnp.bfloat16)
-
-    def to_bins(slot, step):
-        return pltpu.make_async_remote_copy(
-            src_ref=out_ref.at[slot],
-            dst_ref=out_ref.at[slot],
-            send_sem=part_send.at[step],
-            recv_sem=part_recv.at[step],
-            device_id={"bins": lax.rem(place + step, bins)},
-            device_id_type=mesh_ids,
+    far = [mirror_ref[pl.ds(base + part, unit, stride=2), :] for part in range(2)]
+    far_follow = [
+        jnp.where(
+            at_last,
+            after[part : part + 1, :],
+            mirror_ref[pl.ds(base + part + 2, unit, stride=2), :],
         )
-
-    def to_mate(slot, step):
-        return pltpu.make_async_remote_copy(
-            src_ref=out_ref.at[slot],
-            dst_ref=out_ref.at[slot],
-            send_sem=mate_send.at[step],
-            recv_sem=mate_recv.at[step],
-            device_id={"fdot": mate},
-            device_id_type=mesh_ids,
-        )
-
-    sends = [to_bins(mine, step) for step in range(1, bins)] + [to_mate(mine, 0)]
+        for part in range(2)
+    ]
+    far_mirror = [mirror(far[part], far_follow[part]) for part in range(2)]
+    mine = place * WAYS + member
+    near_out = unpack(*own, *far_mirror, own_position, total_bins)
+    far_out = unpack(*far, *own_mirror, far_position, total_bins)
+    for which, values in enumerate((near_out, far_out)):
+        for part in range(2):
+            out_ref[mine, which, part] = (values[part] * scaling).astype(jnp.bfloat16)
+
+    sends = [to_bins(mine, step) for step in range(bins - 1, 0, -1)]
+    sends += [to_across(mine, 0), to_mate(mine, 0)]
     for copy in sends:
         copy.start()
+
+    def block_behind(step):
+        return lax.rem(place + bins - step, bins) * WAYS
+
+    def pass_bins(step):
+        slot = block_behind(step) + member
+        to_bins(slot, step).wait_recv()
+        copies = [to_across(slot, step), to_mate(slot, step)]
+        for copy in copies:
+            copy.start()
+        return copies
+
+    def pass_across(step):
+        slot = block_behind(step) + across_member
+        to_across(slot, step).wait_recv()
+        copy = to_mate(slot, bins + step)
+        copy.start()
+        return [copy]
+
     for step in range(1, bins):
-        slot = lax.rem(place + bins - step, bins) * 2 + side
-        to_bins(slot, step).wait_recv()
-        copy = to_mate(slot, step)
-        copy.start()
-        sends.append(copy)
+        sends += pass_bins(step)
+        sends += pass_across(step - 1)
+    sends += pass_across(bins - 1)
     for step in range(bins):
-        slot = lax.rem(place + bins - step, bins) * 2 + 1 - side
-        to_mate(slot, step).wait_recv()
+        to_mate(block_behind(step) + mate_member, step).wait_recv()
+        to_mate(block_behind(step) + mate_across, bins + step).wait_recv()
     trade.wait_send()
     for copy in tile_copies + sends:
         copy.wait_send()
@@ -166,7 +205,7 @@
 def spread(spectrum):
     bins = lax.axis_size("bins")
     block_rows = spectrum.shape[1] // LANES
-    half = block_rows // 2
+    unit = block_rows // (2 * WAYS)
     lines = spectrum.reshape(2, block_rows, LANES).transpose(1, 0, 2).reshape(2 * block_rows, LANES)
     vmem = pl.BlockSpec(memory_space=pltpu.VMEM)
 
@@ -174,15 +213,18 @@
         spread_kernel(bins, *refs)
 
     dma = pltpu.SemaphoreType.DMA
+    counts = (bins, bins, bins, bins, bins, bins, 2 * bins, 2 * bins)
     return pl.pallas_call(
         kernel,
-        out_shape=jax.ShapeDtypeStruct((2 * bins, 2, half, LANES), jnp.bfloat16),
+        out_shape=jax.ShapeDtypeStruct((WAYS * bins, 2, 2, unit, LANES), jnp.bfloat16),
         in_specs=[vmem],
         out_specs=vmem,
         scratch_shapes=[
-            pltpu.VMEM((2 * half + 16, LANES), jnp.float32),
+            pltpu.VMEM((2 * unit + 16, LANES), jnp.float32),
             pltpu.VMEM((bins, 16, LANES), jnp.float32),
-            dma, dma, dma((bins,)), dma((bins,)), dma((bins,)), dma((bins,)), dma((bins,)), dma((bins,)),
+            dma,
+            dma,
+            *[dma((count,)) for count in counts],
         ],
         compiler_params=pltpu.CompilerParams(collective_id=0, has_side_effects=True),
         name="spread",
@@ -202,8 +244,10 @@
 def search_kernel(block_rows, templates, harm_ref, index_ref, bank_ref, spec_ref, out_ref,
                   lines_ref, window_ref, weight_ref, plane_ref):
     spans, _ = search_layout(block_rows)
-    half = spec_ref.shape[2]
-    total_rows = spec_ref.shape[0] * half
+    bins = spec_ref.shape[0] // WAYS
+    unit = spec_ref.shape[3]
+    half = block_rows // 2
+    total_rows = bins * block_rows
     position = lax.axis_index("bins")
     bank_rows = bank_ref.shape[0]
     lane_of = lax.broadcasted_iota(jnp.int32, (2 * templates, bank_rows), 1)
@@ -234,17 +278,22 @@
         lines_ref[part, :8, :] = jnp.zeros((8, LANES), jnp.float32)
         lines_ref[part, pl.ds(8 + total_rows, 8), :] = jnp.zeros((8, LANES), jnp.float32)
 
-    @pl.loop(0, spec_ref.shape[0])
-    def _(step):
-        row = pl.multiple_of(step * half, half)
-        for part in range(2):
-            lines_ref[part, pl.ds(row + 8, half), :] = pltpu.roll(
-                spec_ref[step, part].astype(jnp.float32), LANES // 2, 1
-            )
+    @pl.loop(0, bins)
+    def _(block):
+        for number in range(2 * WAYS):
+            if number % 2 == 0:
+                slot, which = block * WAYS + number // 2, 0
+            else:
+                slot, which = (bins - 1 - block) * WAYS + (2 * WAYS - 1 - number) // 2, 1
+            row = pl.multiple_of(block * block_rows, block_rows) + (8 + number * unit)
+            for part in range(2):
+                lines_ref[part, pl.ds(row, unit), :] = pltpu.roll(
+                    spec_ref[slot, which, part].astype(jnp.float32), LANES // 2, 1
+                )
 
     low_half = lax.broadcasted_iota(jnp.int32, (half, LANES), 1) < LANES // 2
 
-    @pl.loop(0, spec_ref.shape[0])
+    @pl.loop(0, total_rows // half)
     def _(step):
         row = pl.multiple_of(step * half, half)
         target = pl.ds(row, half)
@@ -309,7 +358,7 @@
     own = fdot_index.shape[0]
     templates = -(-own // 8) * 8
     n_bank = bank.shape[0]
-    total_rows = pieces.shape[0] * pieces.shape[2]
+    total_rows = pieces.shape[0] * 2 * pieces.shape[3]
     _, plane_rows = search_layout(block_rows)
     vmem = pl.BlockSpec(memory_space=pltpu.VMEM)
     smem = pl.BlockSpec(memory_space=pltpu.SMEM)

time: 32.9 us -> 34.5 us (1.049)
  Pallas kernels: 32.7 us -> 34.4 us
    pallas_call x1, Pallas kernels: 20.7 us -> 22.6 us  [spread(): pl.pallas_call(kernel, out_shape=jax.ShapeDtypeStruct((WAYS * bins, 2, 2,...]
where the time goes in v3:
time: 34.5 us; the launch traced here: 34.4 us
  Pallas kernels  34.4 us (100%)
    pallas_call x1, Pallas kernels, spread(): pl.pallas_call(kernel, out_shape=jax.ShapeDtypeStruct((WAYS * bins, 2, 2,...  22.6 us
    pallas_call x1, Pallas kernels, search(): pl.pallas_call(kernel, out_shape=jax.ShapeDtypeStruct((block_rows * templ...  11.8 us

profile of v3, /device:TPU:0, one launch (start us, length us, event | category | flops | bytes accessed | tf_op | source)
XLA Modules:
  0.0 34.4 jit_solution(16178227387728838873)
XLA Ops:
  0.0 22.6 %spread.1.refs_3_ = bf16[16,2,2,32,128]{4,3,2,1,0:T(8,128)(2,1)} custom-call(f32[512,128]{1,0:T(8,128)} %bitcast.14), custom_call_target="tpu_custom_call" | custom-call | tf_op jit(solution)/shard_map/spread/pallas_call | solution.py:217
  22.6 11.8 %search.1 = f32[2048,128]{1,0:T(8,128)} custom-call(s32[4,7]{1,0:T(4,128)} %bitcast.16, s32[8]{0:T(128)} %refs_1_.1, bf16[256,128]{1,0:T(8,128)(2,1)} %bitcast.15, bf16[16,2,2,32,128]{4,3,2,1,0:T(8,128)(2,1)} %spread.1.refs_3_), custom_call_target="tpu_custom_call" | custom-call | tf_op jit(solution)/shard_map/search/pallas_call | solution.py:369

commit v4 on v3

--- a/solution.py
+++ b/solution.py
@@ -11,7 +11,7 @@
 STRIDE_TABLE = (4, 2, 6, 1, 3, 5, 7)
 
 
-WAYS = 4
+WAYS = 2
 
 
 def unpack(real_a, imag_a, real_b, imag_b, position, total_bins):
@@ -40,8 +40,7 @@
 
 
 def spread_kernel(bins, spec_ref, out_ref, mirror_ref, tiles_ref, trade_send, trade_recv,
-                  tile_send, tile_recv, part_send, part_recv, side_send, side_recv,
-                  mate_send, mate_recv):
+                  tile_send, tile_recv, part_send, part_recv, mate_send, mate_recv):
     mesh_ids = pl.DeviceIdType.MESH
     block_rows = spec_ref.shape[0] // 2
     unit = block_rows // (2 * WAYS)
@@ -49,13 +48,17 @@
     whole_member = lax.axis_index("fdot")
     member = lax.rem(whole_member, WAYS)
     mate = whole_member + 1 - 2 * lax.rem(member, 2)
-    across = whole_member + 2 - 4 * (member // 2)
     mate_member = member + 1 - 2 * lax.rem(member, 2)
-    across_member = member + 2 - 4 * (member // 2)
-    mate_across = mate_member + 2 - 4 * (mate_member // 2)
     partner = bins - 1 - place
     total_bins = bins * block_rows * LANES
     edge = jnp.where(member == 0, 1, 0)
+
+    barrier = pltpu.get_barrier_semaphore()
+    for step in range(1, bins):
+        pl.semaphore_signal(
+            barrier, inc=1, device_id={"bins": lax.rem(place + step, bins)}, device_id_type=mesh_ids
+        )
+    pl.semaphore_signal(barrier, inc=1, device_id={"fdot": mate}, device_id_type=mesh_ids)
 
     power = jnp.zeros((8, LANES), jnp.float32)
     for first in range(0, 2 * block_rows, 64):
@@ -73,14 +76,7 @@
     tiles_ref[place, 8:, :] = spec_ref[:8, :]
     mirror_ref[2 * unit + 8 :, :] = jnp.zeros((8, LANES), jnp.float32)
 
-    barrier = pltpu.get_barrier_semaphore()
-    for step in range(1, bins):
-        pl.semaphore_signal(
-            barrier, inc=1, device_id={"bins": lax.rem(place + step, bins)}, device_id_type=mesh_ids
-        )
-    for other in (mate, across):
-        pl.semaphore_signal(barrier, inc=1, device_id={"fdot": other}, device_id_type=mesh_ids)
-    pl.semaphore_wait(barrier, bins + 1)
+    pl.semaphore_wait(barrier, bins)
 
     low = 2 * unit * member
     high = block_rows - unit - low
@@ -117,9 +113,6 @@
     def to_bins(slot, step):
         device = {"bins": lax.rem(place + step, bins)}
         return piece_copy(slot, step, part_send, part_recv, device)
-
-    def to_across(slot, step):
-        return piece_copy(slot, step, side_send, side_recv, {"fdot": across})
 
     def to_mate(slot, step):
         return piece_copy(slot, step, mate_send, mate_recv, {"fdot": mate})
@@ -168,35 +161,21 @@
             out_ref[mine, which, part] = (values[part] * scaling).astype(jnp.bfloat16)
 
     sends = [to_bins(mine, step) for step in range(bins - 1, 0, -1)]
-    sends += [to_across(mine, 0), to_mate(mine, 0)]
+    sends.append(to_mate(mine, 0))
     for copy in sends:
         copy.start()
 
     def block_behind(step):
         return lax.rem(place + bins - step, bins) * WAYS
 
-    def pass_bins(step):
+    for step in range(1, bins):
         slot = block_behind(step) + member
         to_bins(slot, step).wait_recv()
-        copies = [to_across(slot, step), to_mate(slot, step)]
-        for copy in copies:
-            copy.start()
-        return copies
-
-    def pass_across(step):
-        slot = block_behind(step) + across_member
-        to_across(slot, step).wait_recv()
-        copy = to_mate(slot, bins + step)
+        copy = to_mate(slot, step)
         copy.start()
-        return [copy]
-
-    for step in range(1, bins):
-        sends += pass_bins(step)
-        sends += pass_across(step - 1)
-    sends += pass_across(bins - 1)
+        sends.append(copy)
     for step in range(bins):
         to_mate(block_behind(step) + mate_member, step).wait_recv()
-        to_mate(block_behind(step) + mate_across, bins + step).wait_recv()
     trade.wait_send()
     for copy in tile_copies + sends:
         copy.wait_send()
@@ -213,10 +192,9 @@
         spread_kernel(bins, *refs)
 
     dma = pltpu.SemaphoreType.DMA
-    counts = (bins, bins, bins, bins, bins, bins, 2 * bins, 2 * bins)
     return pl.pallas_call(
         kernel,
-        out_shape=jax.ShapeDtypeStruct((WAYS * bins, 2, 2, unit, LANES), jnp.bfloat16),
+        out_shape=pltpu.VMEM((WAYS * bins, 2, 2, unit, LANES), jnp.bfloat16),
         in_specs=[vmem],
         out_specs=vmem,
         scratch_shapes=[
@@ -224,9 +202,10 @@
             pltpu.VMEM((bins, 16, LANES), jnp.float32),
             dma,
             dma,
-            *[dma((count,)) for count in counts],
+            *[dma((bins,)) for _ in range(6)],
         ],
-        compiler_params=pltpu.CompilerParams(collective_id=0, has_side_effects=True),
+        compiler_params=pltpu.CompilerParams(collective_id=0, has_side_effects=True, vmem_limit_bytes=16 * 1024 * 1024
+        ),
         name="spread",
     )(lines)
 
@@ -377,7 +356,7 @@
             pltpu.VMEM((templates, 4 * LANES, 2 * LANES), jnp.bfloat16),
             pltpu.VMEM((plane_rows * templates, LANES), jnp.float32),
         ],
-        compiler_params=pltpu.CompilerParams(vmem_limit_bytes=56 * 1024 * 1024),
+        compiler_params=pltpu.CompilerParams(vmem_limit_bytes=40 * 1024 * 1024),
         name="search",
     )(harm_map[:, 0, :].T, fdot_index, bank.reshape(2 * n_bank, LANES), pieces)
     out = out.reshape(block_rows, templates, LANES).transpose(1, 0, 2)
@@ -386,6 +365,7 @@
 
 def body(spectrum, bank, fdot_index, harm_map):
     pieces = spread(spectrum)
+    pieces = pltpu.with_memory_space_constraint(pieces, pltpu.VMEM)
     return search(pieces, bank, fdot_index, harm_map, spectrum.shape[1] // LANES)
 
 

time: 34.5 us -> 29.8 us (0.86)
  Pallas kernels: 34.4 us -> 28.7 us
  local copies, waits for them, and re-layouts: 0 us -> 0.96 us
    pallas_call x1, Pallas kernels: 22.6 us -> 17.4 us  [spread(): pl.pallas_call(kernel, out_shape=pltpu.VMEM((WAYS * bins, 2, 2, unit, LAN...]
    unnamed x0 -> x8, local copies, waits for them, and re-layouts: none -> 0.96 us
    pallas_call x1, Pallas kernels: 11.8 us -> 11.2 us  [search(): pl.pallas_call(kernel, out_shape=jax.ShapeDtypeStruct((block_rows * templ...]
where the time goes in v4:
time: 29.8 us; the launch traced here: 29.7 us
  Pallas kernels  28.7 us (96%)
  local copies, waits for them, and re-layouts  0.96 us (3%)
    pallas_call x1, Pallas kernels, spread(): pl.pallas_call(kernel, out_shape=pltpu.VMEM((WAYS * bins, 2, 2, unit, LAN...  17.4 us
    pallas_call x1, Pallas kernels, search(): pl.pallas_call(kernel, out_shape=jax.ShapeDtypeStruct((block_rows * templ...  11.2 us
    unnamed x8, local copies, waits for them, and re-layouts  0.96 us

profile of v4, /device:TPU:0, one launch (start us, length us, event | category | flops | bytes accessed | tf_op | source)
XLA Modules:
  0.0 29.7 jit_solution(8655973122867149600)
XLA Ops:
  0.0 0.0 copy-start
  0.0 0.9 %copy-done = f32[2,32768]{1,0:T(2,128)S(1)} copy-done((f32[2,32768]{1,0:T(2,128)S(1)}, f32[2,32768]{1,0:T(2,128)}, u32[]{:S(2)}) %copy-start) | copy-done | bytes 262168
  1.0 0.0 copy-start.1
  1.0 0.0 copy-start.2
  1.0 0.0 copy-start.3
  1.0 17.4 %spread.1.refs_3_ = bf16[8,2,2,64,128]{4,3,2,1,0:T(8,128)(2,1)S(1)} custom-call(f32[512,128]{1,0:T(8,128)S(1)} %bitcast.14), custom_call_target="tpu_custom_call" | custom-call | tf_op jit(solution)/shard_map/spread/pallas_call | solution.py:195
  18.4 0.0 copy-done.1
  18.4 0.0 copy-done.2
  18.4 0.0 copy-done.3
  18.4 11.2 %search.1 = f32[2048,128]{1,0:T(8,128)} custom-call(s32[4,7]{1,0:T(4,128)S(1)} %bitcast.16, s32[8]{0:T(128)S(1)} %copy-done.3, bf16[256,128]{1,0:T(8,128)(2,1)S(1)} %bitcast.15, bf16[8,2,2,64,128]{4,3,2,1,0:T(8,128)(2,1)S(1)} %spread.1.refs_3_), custom_call_target="tpu_custom_call" | custom-call | tf_op jit(solution)/shard_map/search/pallas_call | solution.py:348
Async XLA Ops:
  0.0 0.9 %copy-start = (f32[2,32768]{1,0:T(2,128)S(1)}, f32[2,32768]{1,0:T(2,128)}, u32[]{:S(2)}) copy-start(f32[2,32768]{1,0:T(2,128)} %param.4) | copy-start | bytes 786436
  1.0 17.5 %copy-start.1 = (bf16[128,2,128]{2,1,0:T(2,128)(2,1)S(1)}, bf16[128,2,128]{2,1,0:T(2,128)(2,1)}, u32[]{:S(2)}) copy-start(bf16[128,2,128]{2,1,0:T(2,128)(2,1)} %param.5) | copy-start | bytes 196612
  1.0 17.5 %copy-start.2 = (s32[7,1,4]{0,2,1:T(4,128)S(1)}, s32[7,1,4]{0,2,1:T(4,128)}, u32[]{:S(2)}) copy-start(s32[7,1,4]{0,2,1:T(4,128)} %param.7) | copy-start | bytes 340
  1.0 17.5 %copy-start.3 = (s32[8]{0:T(128)S(1)}, s32[8]{0:T(128)}, u32[]{:S(2)}) copy-start(s32[8]{0:T(128)} %refs_1_.1) | copy-start | bytes 100

commit v5 on v4

--- a/solution.py
+++ b/solution.py
@@ -287,7 +287,7 @@
                 low_half, here, after
             ).astype(jnp.bfloat16)
 
-    @pl.loop(0, templates)
+    @pl.loop(0, templates, unroll=2)
     def _(template):
         weight = weight_ref[template]
         for stride, first, count in spans:
@@ -301,7 +301,7 @@
             )
 
     column = lax.broadcasted_iota(jnp.int32, (templates, LANES), 1)
-    wide = 8
+    wide = 16
     bases = [
         (column * stride + harm_ref[3, number]) >> 3 for number, stride in enumerate(STRIDE_TABLE)
     ]

time: 29.8 us -> 28.5 us (0.956)
  Pallas kernels: 28.7 us -> 27.4 us
    pallas_call x1, Pallas kernels: 11.2 us -> 9.92 us  [search(): pl.pallas_call(kernel, out_shape=jax.ShapeDtypeStruct((block_rows * templ...]
where the time goes in v5:
time: 28.5 us; the launch traced here: 28.4 us
  Pallas kernels  27.4 us (96%)
  local copies, waits for them, and re-layouts  0.96 us (3%)
    pallas_call x1, Pallas kernels, spread(): pl.pallas_call(kernel, out_shape=pltpu.VMEM((WAYS * bins, 2, 2, unit, LAN...  17.4 us
    pallas_call x1, Pallas kernels, search(): pl.pallas_call(kernel, out_shape=jax.ShapeDtypeStruct((block_rows * templ...  9.92 us
    unnamed x8, local copies, waits for them, and re-layouts  0.96 us

profile of v5, /device:TPU:0, one launch (start us, length us, event | category | flops | bytes accessed | tf_op | source)
XLA Modules:
  0.0 28.4 jit_solution(5213376518648629823)
XLA Ops:
  0.0 0.0 copy-start
  0.0 0.9 %copy-done = f32[2,32768]{1,0:T(2,128)S(1)} copy-done((f32[2,32768]{1,0:T(2,128)S(1)}, f32[2,32768]{1,0:T(2,128)}, u32[]{:S(2)}) %copy-start) | copy-done | bytes 262168
  1.0 0.0 copy-start.1
  1.0 0.0 copy-start.2
  1.0 0.0 copy-start.3
  1.0 17.4 %spread.1.refs_3_ = bf16[8,2,2,64,128]{4,3,2,1,0:T(8,128)(2,1)S(1)} custom-call(f32[512,128]{1,0:T(8,128)S(1)} %bitcast.14), custom_call_target="tpu_custom_call" | custom-call | tf_op jit(solution)/shard_map/spread/pallas_call | solution.py:195
  18.4 0.0 copy-done.1
  18.4 0.0 copy-done.2
  18.4 0.0 copy-done.3
  18.4 9.9 %search.1 = f32[2048,128]{1,0:T(8,128)} custom-call(s32[4,7]{1,0:T(4,128)S(1)} %bitcast.16, s32[8]{0:T(128)S(1)} %copy-done.3, bf16[256,128]{1,0:T(8,128)(2,1)S(1)} %bitcast.15, bf16[8,2,2,64,128]{4,3,2,1,0:T(8,128)(2,1)S(1)} %spread.1.refs_3_), custom_call_target="tpu_custom_call" | custom-call | tf_op jit(solution)/shard_map/search/pallas_call | solution.py:348
Async XLA Ops:
  0.0 0.9 %copy-start = (f32[2,32768]{1,0:T(2,128)S(1)}, f32[2,32768]{1,0:T(2,128)}, u32[]{:S(2)}) copy-start(f32[2,32768]{1,0:T(2,128)} %param.4) | copy-start | bytes 786436
  1.0 17.5 %copy-start.1 = (bf16[128,2,128]{2,1,0:T(2,128)(2,1)S(1)}, bf16[128,2,128]{2,1,0:T(2,128)(2,1)}, u32[]{:S(2)}) copy-start(bf16[128,2,128]{2,1,0:T(2,128)(2,1)} %param.5) | copy-start | bytes 196612
  1.0 17.5 %copy-start.2 = (s32[7,1,4]{0,2,1:T(4,128)S(1)}, s32[7,1,4]{0,2,1:T(4,128)}, u32[]{:S(2)}) copy-start(s32[7,1,4]{0,2,1:T(4,128)} %param.7) | copy-start | bytes 340
  1.0 17.5 %copy-start.3 = (s32[8]{0:T(128)S(1)}, s32[8]{0:T(128)}, u32[]{:S(2)}) copy-start(s32[8]{0:T(128)} %refs_1_.1) | copy-start | bytes 100
